TPU v7x, 32 devices: a whole 2x2x4 slice. The times are simulated.
32 devices in a mesh: seq: 8 (over z, y), mp: 2 (over x), dp: 2 (over core).
Axes of the slice: x: 2, y: 2, z: 4, core: 2. Of those that a mesh axis runs over, the one named last changes fastest.
Arguments:
- encoder_hidden: bfloat16 [2, 896, 4096], P('dp', 'seq'), may hold values from -6 to 6
- kv_weight: bfloat16 [4096, 2, 2048], P(None, None, 'mp')
- self_proj: bfloat16 [2, 512, 3, 2048], P('dp', 'seq', None, 'mp'), may hold values from -20 to 20
- cross_query: bfloat16 [2, 512, 2048], P('dp', 'seq', 'mp'), may hold values from -12 to 12
- cotangents: bfloat16 [2, 512, 2, 2048], P('dp', 'seq', None, 'mp'), may hold values from -6 to 6
- position_bias: float32 [8, 8], replicated, may hold values from -4 to 4
- input_lengths: int32 [2, 8, 8], P('dp', 'seq'), may hold values from 1 to 32, 112 in all within a row
- target_home: int32 [2, 8, 8], P('dp', 'seq'), may hold values from 0 to 7, each once within a row
- target_lengths: int32 [2, 8, 8], P('dp', 'seq'), may hold values from 1 to 8, 40 in all within a row
- drop_seed: int32 [1], replicated, may hold values from 0 to 999999
Outputs:
- cross_output: bfloat16 [2, 512, 2048], P('dp', 'seq', 'mp')
- self_output: bfloat16 [2, 512, 2048], P('dp', 'seq', 'mp')
- decoder_grads: bfloat16 [2, 512, 4, 2048], P('dp', 'seq', None, 'mp')
- hidden_grads: bfloat16 [2, 896, 4096], P('dp', 'seq', 'mp')
- position_grad: float32 [8, 8], replicated
Inputs may be any that keep to these rules, and one draw needn't show every extreme that they name: `input_lengths`: each encoder shard sends exactly one example to each decoder shard; the input lengths of one shard fill its 112 rows, and some example has exactly 32. `target_home`: per encoder shard, each decoder shard is named once. `target_lengths`: the target lengths of one decoder shard sum to 40, and some slot has exactly 8.
All inputs are finite; a program needn't handle non-finite values.
Results may differ from a plain program's by a relative error of at most 0.004.
The roundings to bfloat16 on the way count: a program that leaves them out, or rounds other values in their place, can miss the bound.
Values may be sent and summed in bfloat16 or wider, within the bound.
A program may use at most 64 MiB of HBM per device.

v0:
```python
import functools

import jax
import jax.numpy as jnp
from jax import lax
from jax.experimental import pallas as pl
from jax.experimental.pallas import tpu as pltpu
from jax.sharding import PartitionSpec as P

HEAD = 256
TGT_MAX = 8
PIECES = 4
STAGE = 256
DEPTH = 4

MESH = pl.DeviceIdType.MESH
drop_limit = 6554
keep_factor = 65536.0 / (65536.0 - 6554.0)


def scramble(state):
    state = state ^ ((state >> 16) & 65535)
    state = state * 73244475
    state = state ^ ((state >> 16) & 65535)
    state = state * 73244475
    state = state ^ ((state >> 16) & 65535)
    return state


def keep_table(base, head, query_pos, key_pos):
    state = scramble(base + head)
    state = scramble(state + query_pos)
    state = scramble(state + key_pos)
    return jnp.where((state & 65535) >= drop_limit, keep_factor, 0.0).astype(jnp.float32)


def nt(a, b):
    return lax.dot_general(a, b, (((1,), (1,)), ((), ())), preferred_element_type=jnp.float32)


def nn(a, b):
    return lax.dot_general(a, b, (((1,), (0,)), ((), ())), preferred_element_type=jnp.float32)


def tn(a, b):
    return lax.dot_general(a, b, (((0,), (0,)), ((), ())), preferred_element_type=jnp.float32)


def softmax(scores):
    peak = jnp.max(scores, axis=-1, keepdims=True)
    expo = jnp.exp(scores - peak)
    return expo / jnp.sum(expo, axis=-1, keepdims=True)


def kernel(
    sizes,
    lengths_in,
    homes_in,
    counts_in,
    seed_in,
    bias_in,
    hidden_in,
    weight,
    self_in,
    query_in,
    cotangents_in,
    self_out,
    cross_out,
    decoder_grads,
    hidden_out,
    position_out,
    lengths,
    homes,
    counts,
    seed,
    bias,
    hidden,
    self_proj,
    cross_query,
    cotangents,
    stage,
    w_buf,
    kv_acc,
    kv_buf,
    grad_buf,
    self_grad,
    planes,
    sent,
    got,
    reply,
    got_reply,
    partial_send,
    partial_got,
    pos_seq,
    pos_all,
    w_sem,
    x_send,
    x_recv,
    r_send,
    r_recv,
    h_send,
    h_recv,
    p_send,
    p_recv,
    a_send,
    a_recv,
    in_sem,
):
    seq, mp, dp = sizes
    me = lax.axis_index("seq")
    column = lax.axis_index("mp")
    group = lax.axis_index("dp")
    enc = hidden.shape[0]
    model = hidden.shape[1]
    dec, features = cross_query.shape
    heads = features // HEAD
    factor = HEAD ** (-0.5)
    rows2 = 2 * TGT_MAX
    others = mp * dp
    mine = column * dp + group
    steps = model // STAGE

    def w_copy(n):
        slot = lax.rem(n, DEPTH)
        return pltpu.make_async_copy(
            weight.at[pl.ds(n * STAGE, STAGE)], stage.at[slot], w_sem.at[slot]
        )

    def other_id(k):
        other = lax.rem(mine + k, others)
        return {"mp": other // dp, "dp": lax.rem(other, dp)}

    barrier = pltpu.get_barrier_semaphore()
    for k in range(1, seq):
        pl.semaphore_signal(
            barrier, inc=1, device_id={"seq": lax.rem(me + k, seq)}, device_id_type=MESH
        )

    def greet(k, carry):
        pl.semaphore_signal(barrier, inc=1, device_id=other_id(k), device_id_type=MESH)
        return carry

    lax.fori_loop(1, others, greet, 0)
    incoming = [
        pltpu.make_async_copy(source, target, in_sem.at[i])
        for i, (source, target) in enumerate(
            (
                (counts_in, counts),
                (query_in, cross_query),
                (cotangents_in, cotangents),
                (hidden_in, hidden),
                (lengths_in, lengths),
                (homes_in, homes),
                (seed_in, seed),
                (bias_in, bias),
                (self_in, self_proj),
            )
        )
    ]
    for copy in incoming:
        copy.start()
    for n in range(DEPTH):
        w_copy(jnp.int32(n)).start()
    for copy in incoming[:3]:
        copy.wait()

    def pick(value, which):
        return value.reshape(seq, 2, TGT_MAX, value.shape[1])[:, which].reshape(
            dec, value.shape[1]
        )

    def mix(first, second):
        shape = (seq, 1, TGT_MAX, first.shape[1])
        return jnp.concatenate([first.reshape(shape), second.reshape(shape)], axis=1).reshape(
            2 * dec, first.shape[1]
        )

    def live_rows(width):
        row = lax.broadcasted_iota(jnp.int32, (dec, width), 0)
        count = jnp.zeros((dec, width), jnp.int32)
        for s in range(seq):
            count = jnp.where((row >> 3) == s, counts[s], count)
        return (row & 7) < count

    both_grads = jnp.swapaxes(cotangents[...], 0, 1)
    self_grad[...] = both_grads[0]
    cross_grad = jnp.where(live_rows(features), both_grads[1].astype(jnp.float32), 0.0)
    sent[...] = mix(cross_query[...].astype(jnp.float32), cross_grad).astype(jnp.bfloat16)
    pl.semaphore_wait(barrier, seq - 1 + others - 1)

    def slot(ref, index):
        return ref.at[pl.ds(pl.multiple_of(index * rows2, rows2), rows2), :]

    def x_copy(k):
        to = lax.rem(me + k, seq)
        return pltpu.make_async_remote_copy(
            src_ref=slot(sent, to),
            dst_ref=slot(got, me),
            send_sem=x_send.at[k],
            recv_sem=x_recv.at[k],
            device_id={"seq": to},
            device_id_type=MESH,
        )

    def r_copy(k):
        to = lax.rem(me + k, seq)
        return pltpu.make_async_remote_copy(
            src_ref=slot(reply, to),
            dst_ref=slot(got_reply, me),
            send_sem=r_send.at[k],
            recv_sem=r_recv.at[k],
            device_id={"seq": to},
            device_id_type=MESH,
        )

    def p_copy(k):
        return pltpu.make_async_remote_copy(
            src_ref=pos_seq.at[me],
            dst_ref=pos_seq.at[me],
            send_sem=p_send.at[k],
            recv_sem=p_recv.at[k],
            device_id={"seq": lax.rem(me + k, seq)},
            device_id_type=MESH,
        )

    def a_copy(k):
        return pltpu.make_async_remote_copy(
            src_ref=pos_all.at[mine],
            dst_ref=pos_all.at[mine],
            send_sem=a_send.at[k],
            recv_sem=a_recv.at[k],
            device_id=other_id(k),
            device_id_type=MESH,
        )

    for k in range(1, seq):
        x_copy(k).start()
    own_rows = pl.ds(pl.multiple_of(me * rows2, rows2), rows2)
    got[own_rows, :] = sent[own_rows, :]

    kv_acc[...] = jnp.zeros_like(kv_acc)
    for copy in incoming[3:]:
        copy.wait()

    def project(n, carry):
        w_copy(n).wait()
        rows = pl.ds(pl.multiple_of(n * STAGE, STAGE), STAGE)
        part = jnp.swapaxes(stage[lax.rem(n, DEPTH)], 0, 1)
        w_buf[:, rows, :] = part
        left = hidden[:, rows]
        kv_acc[0] += nn(left, part[0])
        kv_acc[1] += nn(left, part[1])

        @pl.when(n + DEPTH < steps)
        def _():
            w_copy(n + DEPTH).start()

        return carry

    lax.fori_loop(0, steps, project, 0)
    kv_buf[...] = kv_acc[...].astype(jnp.bfloat16)

    for k in range(1, seq):
        x_copy(k).wait()

    row = lax.broadcasted_iota(jnp.int32, (dec, enc), 0)
    col = lax.broadcasted_iota(jnp.int32, (dec, enc), 1)
    home = jnp.zeros((dec, enc), jnp.int32)
    offset = jnp.int32(0)
    for e in range(seq):
        home = jnp.where(col >= offset, homes[e], home)
        offset = offset + lengths[e]
    allowed = (row >> 3) == home
    query_pos = (row >> 3) * dec + me * TGT_MAX + (row & 7)
    key_pos = me * enc + col
    base = scramble(seed[0] + group * 104729)
    blank = jnp.zeros((dec, enc), jnp.float32)
    for h in range(heads):
        cols = slice(h * HEAD, (h + 1) * HEAD)
        head = column * heads + h
        both = got[:, cols]
        key, val = kv_buf[0, :, cols], kv_buf[1, :, cols]
        probs = softmax(jnp.where(allowed, pick(nt(both, key), 0) * factor, -1e30))
        keep = keep_table(base, head, query_pos, key_pos)
        weights = probs * keep
        dprobs = pick(nt(both, val), 1) * keep
        delta = jnp.sum(probs * dprobs, axis=-1, keepdims=True)
        scaled = probs * (dprobs - delta) * factor
        grad_buf[0, :, cols] = tn(mix(scaled, blank).astype(jnp.bfloat16), both).astype(
            jnp.bfloat16
        )
        grad_buf[1, :, cols] = tn(mix(blank, weights).astype(jnp.bfloat16), both).astype(
            jnp.bfloat16
        )
        reply[:, cols] = mix(
            nn(weights.astype(jnp.bfloat16), val), nn(scaled.astype(jnp.bfloat16), key)
        ).astype(jnp.bfloat16)

    share = model // mp
    piece = share // PIECES

    def product(begin):
        rows = pl.ds(begin, piece)
        total = nt(grad_buf[0], w_buf[0, rows, :]) + nt(grad_buf[1], w_buf[1, rows, :])
        return total.astype(jnp.bfloat16)

    def h_copy(k, i):
        return pltpu.make_async_remote_copy(
            src_ref=partial_send.at[k, i],
            dst_ref=partial_got.at[column, i],
            send_sem=h_send.at[k, i],
            recv_sem=h_recv.at[k, i],
            device_id={"mp": lax.rem(column + k, mp)},
            device_id_type=MESH,
        )

    for k in range(1, mp):
        to = lax.rem(column + k, mp)

        def send_piece(i, carry, k=k, to=to):
            partial_send[k, i] = product(pl.multiple_of(to * share + i * piece, piece))
            h_copy(k, i).start()
            return carry

        lax.fori_loop(0, PIECES, send_piece, 0)

    for k in range(1, seq):
        r_copy(k).start()
    got_reply[own_rows, :] = reply[own_rows, :]

    row = lax.broadcasted_iota(jnp.int32, (dec, dec), 0)
    col = lax.broadcasted_iota(jnp.int32, (dec, dec), 1)
    count = jnp.zeros((dec, dec), jnp.int32)
    for s in range(seq):
        count = jnp.where((row >> 3) == s, counts[s], count)
    distance = row - col
    allowed = ((row >> 3) == (col >> 3)) & (distance >= 0) & ((col & 7) < count)
    live = (row & 7) < count
    base = scramble(seed[0] + 7919 + group * 104729)
    lane = lax.broadcasted_iota(jnp.int32, (TGT_MAX, 128), 1)
    position = jnp.zeros((TGT_MAX, 128), jnp.float32)
    for h in range(heads):
        cols = slice(h * HEAD, (h + 1) * HEAD)
        head = column * heads + h
        q, key, val = self_proj[0, :, cols], self_proj[1, :, cols], self_proj[2, :, cols]
        grad = self_grad[:, cols]
        shift = jnp.zeros((dec, dec), jnp.float32)
        for r in range(TGT_MAX):
            shift = jnp.where(distance == r, bias[r, head], shift)
        probs = softmax(jnp.where(allowed, nt(q, key) * factor + shift, -1e30))
        keep = keep_table(base, head, me * dec + row, me * dec + col)
        weights = jnp.where(live, probs * keep, 0.0).astype(jnp.bfloat16)
        self_out[:, cols] = nn(weights, val).astype(jnp.bfloat16)
        dprobs = nt(grad, val) * keep
        delta = jnp.sum(probs * dprobs, axis=-1, keepdims=True)
        dscores = jnp.where(live, probs * (dprobs - delta), 0.0)
        scaled = (dscores * factor).astype(jnp.bfloat16)
        planes[0, :, cols] = nn(scaled, key).astype(jnp.bfloat16)
        planes[1, :, cols] = tn(scaled, q).astype(jnp.bfloat16)
        planes[2, :, cols] = tn(weights, grad).astype(jnp.bfloat16)
        sums = jnp.concatenate(
            [
                jnp.sum(jnp.where(distance == r, dscores, 0.0), axis=0, keepdims=True)
                for r in range(TGT_MAX)
            ],
            axis=0,
        )
        total = jnp.sum(sums, axis=1, keepdims=True)
        position = jnp.where(lane == head, total, position)
    pos_seq[me] = position

    def keep_piece(i, carry):
        partial_got[column, i] = product(pl.multiple_of(column * share + i * piece, piece))
        return carry

    lax.fori_loop(0, PIECES - 1, keep_piece, 0)

    for k in range(1, seq):
        p_copy(k).start()
    lax.fori_loop(PIECES - 1, PIECES, keep_piece, 0)
    for k in range(1, seq):
        p_copy(k).wait()
    total = pos_seq[0]
    for s in range(1, seq):
        total = total + pos_seq[s]
    pos_all[mine] = total

    for k in range(1, seq):
        r_copy(k).wait()
    back = got_reply[...].astype(jnp.float32)
    cross_out[...] = jnp.where(live_rows(features), pick(back, 0), 0.0).astype(jnp.bfloat16)
    planes[3] = pick(back, 1).astype(jnp.bfloat16)
    decoder_grads[...] = jnp.swapaxes(planes[...], 0, 1)

    def share_total(k, carry):
        a_copy(k).start()
        return carry

    lax.fori_loop(1, others, share_total, 0)

    for i in range(PIECES):
        for k in range(1, mp):
            h_copy(k, i).wait()
        total = partial_got[0, i].astype(jnp.float32)
        for m in range(1, mp):
            total = total + partial_got[m, i].astype(jnp.float32)
        hidden_out[:, i * piece : (i + 1) * piece] = total.astype(jnp.bfloat16)

    def take_total(k, carry):
        a_copy(k).wait()
        return carry

    lax.fori_loop(1, others, take_total, 0)
    total = pos_all[0]
    for m in range(1, others):
        total = total + pos_all[m]
    position_out[...] = total


def deliver(*refs):
    taken, given, done = refs[:5], refs[5:10], refs[10]
    copies = [pltpu.make_async_copy(taken[i], given[i], done.at[i]) for i in range(4)]
    for copy in copies:
        copy.start()
    given[4][...] = taken[4][:, : given[4].shape[1]]
    for copy in copies:
        copy.wait()


def body(
    sizes,
    encoder_hidden,
    kv_weight,
    self_proj,
    cross_query,
    cotangents,
    position_bias,
    input_lengths,
    target_home,
    target_lengths,
    drop_seed,
):
    seq, mp, dp = sizes
    enc, model = encoder_hidden.shape[1:]
    dec, features = cross_query.shape[1:]
    share = model // mp
    others = mp * dp
    vmem = pl.BlockSpec(memory_space=pltpu.VMEM)
    far = pl.BlockSpec(memory_space=pltpu.HBM)
    hbm = pl.BlockSpec(memory_space=pl.ANY)
    half = jnp.bfloat16
    dma = pltpu.SemaphoreType.DMA
    shapes = [
        jax.ShapeDtypeStruct((dec, features), half),
        jax.ShapeDtypeStruct((dec, features), half),
        jax.ShapeDtypeStruct((dec, 4, features), half),
        jax.ShapeDtypeStruct((enc, share), half),
        jax.ShapeDtypeStruct((TGT_MAX, 128), jnp.float32),
    ]
    results = pl.pallas_call(
        functools.partial(kernel, sizes),
        out_shape=tuple(shapes),
        in_specs=[far] * 10,
        out_specs=(vmem,) * 5,
        scratch_shapes=[
            pltpu.SMEM((seq,), jnp.int32),
            pltpu.SMEM((seq,), jnp.int32),
            pltpu.SMEM((seq,), jnp.int32),
            pltpu.SMEM((1,), jnp.int32),
            pltpu.SMEM(position_bias.shape, jnp.float32),
            pltpu.VMEM((enc, model), half),
            pltpu.VMEM((3, dec, features), half),
            pltpu.VMEM((dec, features), half),
            pltpu.VMEM((dec, 2, features), half),
            pltpu.VMEM((DEPTH, STAGE, 2, features), half),
            pltpu.VMEM((2, model, features), half),
            pltpu.VMEM((2, enc, features), jnp.float32),
            pltpu.VMEM((2, enc, features), half),
            pltpu.VMEM((2, enc, features), half),
            pltpu.VMEM((dec, features), half),
            pltpu.VMEM((4, dec, features), half),
            pltpu.VMEM((2 * dec, features), half),
            pltpu.VMEM((2 * dec, features), half),
            pltpu.VMEM((2 * dec, features), half),
            pltpu.VMEM((2 * dec, features), half),
            pltpu.VMEM((mp, PIECES, enc, share // PIECES), half),
            pltpu.VMEM((mp, PIECES, enc, share // PIECES), half),
            pltpu.VMEM((seq, TGT_MAX, 128), jnp.float32),
            pltpu.VMEM((others, TGT_MAX, 128), jnp.float32),
            dma((DEPTH,)),
            dma((seq,)),
            dma((seq,)),
            dma((seq,)),
            dma((seq,)),
            dma((mp, PIECES)),
            dma((mp, PIECES)),
            dma((seq,)),
            dma((seq,)),
            dma((others,)),
            dma((others,)),
            dma((9,)),
        ],
        compiler_params=pltpu.CompilerParams(
            collective_id=0, has_side_effects=True, vmem_limit_bytes=67043328
        ),
        name="fused_layer",
    )(
        input_lengths.reshape(seq),
        target_home.reshape(seq),
        target_lengths.reshape(seq),
        drop_seed,
        position_bias,
        encoder_hidden[0],
        kv_weight,
        jnp.swapaxes(self_proj[0], 0, 1),
        cross_query[0],
        cotangents[0],
    )
    shapes[4] = jax.ShapeDtypeStruct(position_bias.shape, jnp.float32)
    self_out, cross_out, decoder_grads, hidden_out, position_out = pl.pallas_call(
        deliver,
        out_shape=tuple(shapes),
        in_specs=[vmem] * 5,
        out_specs=(hbm,) * 4 + (vmem,),
        scratch_shapes=[dma((4,))],
        compiler_params=pltpu.CompilerParams(vmem_limit_bytes=67043328),
        name="deliver",
    )(*results)
    return (
        cross_out[None],
        self_out[None],
        decoder_grads[None],
        hidden_out[None],
        position_out,
    )


def solution(mesh):
    sizes = (mesh.shape["seq"], mesh.shape["mp"], mesh.shape["dp"])
    placed = (
        P("dp", "seq", None),
        P(None, None, "mp"),
        P("dp", "seq", None, "mp"),
        P("dp", "seq", "mp"),
        P("dp", "seq", None, "mp"),
        P(),
        P("dp", "seq", None),
        P("dp", "seq", None),
        P("dp", "seq", None),
        P(),
    )
    return jax.shard_map(
        functools.partial(body, sizes),
        mesh=mesh,
        in_specs=placed,
        out_specs=(
            P("dp", "seq", "mp"),
            P("dp", "seq", "mp"),
            P("dp", "seq", None, "mp"),
            P("dp", "seq", "mp"),
            P(),
        ),
        check_vma=False,
    )
```

profile of v0, /device:TPU:0, one launch (start us, length us, event | category | flops | bytes accessed | tf_op | source)
XLA Modules:
  0.0 38.8 jit_solution(6729517785510887322)
XLA Ops:
  1.3 34.6 %fused_layer.1 = (bf16[64,1024]{1,0:T(8,128)(2,1)}, bf16[64,1024]{1,0:T(8,128)(2,1)}, bf16[64,4,1024]{2,1,0:T(4,128)(2,1)}, bf16[112,2048]{1,0:T(8,128)(2,1)}, f32[8,128]{1,0:T(8,128)}) custom-call(s32[8]{0:T(128)} %bitcast.17, s32[8]{0:T(128)} %bitcast.18, s32[8]{0:T(128)} %bitcast.19, s32[1]{0:T(128)S(6)} %copy.15.seed_in, f32[8,8]{1,0:T(8,128)} %bias_in.1, ...), custom_call_target="tpu_custom_call" | custom-call | tf_op jit(solution)/shard_map/fused_layer/pallas_call | solution.py:460
  35.9 2.9 %deliver.1 = (bf16[64,1024]{1,0:T(8,128)(2,1)}, bf16[64,1024]{1,0:T(8,128)(2,1)}, bf16[64,4,1024]{2,1,0:T(4,128)(2,1)}, bf16[112,2048]{1,0:T(8,128)(2,1)}, f32[8,8]{1,0:T(8,128)}) custom-call(bf16[64,1024]{1,0:T(8,128)(2,1)} %get-tuple-element.15.refs_0_, bf16[64,1024]{1,0:T(8,128)(2,1)} %get-tuple-element.16.refs_1_, ...), custom_call_target="tpu_custom_call" | custom-call | tf_op jit(solution)/shard_map/deliver/pallas_call | solution.py:520
where the time goes:
time: 39 us; the launch traced here: 38.8 us
  Pallas kernels  37.5 us (96%)
  between operations  1.29 us (3%)
    pallas_call x1, Pallas kernels, body(): pl.pallas_call(functools.partial(kernel, sizes), out_shape=tuple(shapes),...  34.6 us
    pallas_call x1, Pallas kernels, body(): pl.pallas_call(deliver, out_shape=tuple(shapes), in_specs=[vmem] * 5, out...  2.95 us

commit v1 on v0

--- a/solution.py
+++ b/solution.py
@@ -9,9 +9,9 @@
 
 HEAD = 256
 TGT_MAX = 8
-PIECES = 4
+PIECES = 8
 STAGE = 256
-DEPTH = 4
+EARLY = 7
 
 MESH = pl.DeviceIdType.MESH
 drop_limit = 6554
@@ -121,9 +121,8 @@
     steps = model // STAGE
 
     def w_copy(n):
-        slot = lax.rem(n, DEPTH)
         return pltpu.make_async_copy(
-            weight.at[pl.ds(n * STAGE, STAGE)], stage.at[slot], w_sem.at[slot]
+            weight.at[pl.ds(n * STAGE, STAGE)], stage.at[n], w_sem.at[n]
         )
 
     def other_id(k):
@@ -148,19 +147,23 @@
                 (counts_in, counts),
                 (query_in, cross_query),
                 (cotangents_in, cotangents),
+                (seed_in, seed),
+                (bias_in, bias),
+                (self_in, self_proj),
                 (hidden_in, hidden),
                 (lengths_in, lengths),
                 (homes_in, homes),
-                (seed_in, seed),
-                (bias_in, bias),
-                (self_in, self_proj),
             )
         )
     ]
     for copy in incoming:
         copy.start()
-    for n in range(DEPTH):
-        w_copy(jnp.int32(n)).start()
+
+    def load(n, carry):
+        w_copy(n).start()
+        return carry
+
+    lax.fori_loop(0, steps, load, 0)
     for copy in incoming[:3]:
         copy.wait()
 
@@ -186,7 +189,6 @@
     self_grad[...] = both_grads[0]
     cross_grad = jnp.where(live_rows(features), both_grads[1].astype(jnp.float32), 0.0)
     sent[...] = mix(cross_query[...].astype(jnp.float32), cross_grad).astype(jnp.bfloat16)
-    pl.semaphore_wait(barrier, seq - 1 + others - 1)
 
     def slot(ref, index):
         return ref.at[pl.ds(pl.multiple_of(index * rows2, rows2), rows2), :]
@@ -233,100 +235,10 @@
             device_id_type=MESH,
         )
 
-    for k in range(1, seq):
-        x_copy(k).start()
     own_rows = pl.ds(pl.multiple_of(me * rows2, rows2), rows2)
     got[own_rows, :] = sent[own_rows, :]
-
-    kv_acc[...] = jnp.zeros_like(kv_acc)
-    for copy in incoming[3:]:
+    for copy in incoming[3:6]:
         copy.wait()
-
-    def project(n, carry):
-        w_copy(n).wait()
-        rows = pl.ds(pl.multiple_of(n * STAGE, STAGE), STAGE)
-        part = jnp.swapaxes(stage[lax.rem(n, DEPTH)], 0, 1)
-        w_buf[:, rows, :] = part
-        left = hidden[:, rows]
-        kv_acc[0] += nn(left, part[0])
-        kv_acc[1] += nn(left, part[1])
-
-        @pl.when(n + DEPTH < steps)
-        def _():
-            w_copy(n + DEPTH).start()
-
-        return carry
-
-    lax.fori_loop(0, steps, project, 0)
-    kv_buf[...] = kv_acc[...].astype(jnp.bfloat16)
-
-    for k in range(1, seq):
-        x_copy(k).wait()
-
-    row = lax.broadcasted_iota(jnp.int32, (dec, enc), 0)
-    col = lax.broadcasted_iota(jnp.int32, (dec, enc), 1)
-    home = jnp.zeros((dec, enc), jnp.int32)
-    offset = jnp.int32(0)
-    for e in range(seq):
-        home = jnp.where(col >= offset, homes[e], home)
-        offset = offset + lengths[e]
-    allowed = (row >> 3) == home
-    query_pos = (row >> 3) * dec + me * TGT_MAX + (row & 7)
-    key_pos = me * enc + col
-    base = scramble(seed[0] + group * 104729)
-    blank = jnp.zeros((dec, enc), jnp.float32)
-    for h in range(heads):
-        cols = slice(h * HEAD, (h + 1) * HEAD)
-        head = column * heads + h
-        both = got[:, cols]
-        key, val = kv_buf[0, :, cols], kv_buf[1, :, cols]
-        probs = softmax(jnp.where(allowed, pick(nt(both, key), 0) * factor, -1e30))
-        keep = keep_table(base, head, query_pos, key_pos)
-        weights = probs * keep
-        dprobs = pick(nt(both, val), 1) * keep
-        delta = jnp.sum(probs * dprobs, axis=-1, keepdims=True)
-        scaled = probs * (dprobs - delta) * factor
-        grad_buf[0, :, cols] = tn(mix(scaled, blank).astype(jnp.bfloat16), both).astype(
-            jnp.bfloat16
-        )
-        grad_buf[1, :, cols] = tn(mix(blank, weights).astype(jnp.bfloat16), both).astype(
-            jnp.bfloat16
-        )
-        reply[:, cols] = mix(
-            nn(weights.astype(jnp.bfloat16), val), nn(scaled.astype(jnp.bfloat16), key)
-        ).astype(jnp.bfloat16)
-
-    share = model // mp
-    piece = share // PIECES
-
-    def product(begin):
-        rows = pl.ds(begin, piece)
-        total = nt(grad_buf[0], w_buf[0, rows, :]) + nt(grad_buf[1], w_buf[1, rows, :])
-        return total.astype(jnp.bfloat16)
-
-    def h_copy(k, i):
-        return pltpu.make_async_remote_copy(
-            src_ref=partial_send.at[k, i],
-            dst_ref=partial_got.at[column, i],
-            send_sem=h_send.at[k, i],
-            recv_sem=h_recv.at[k, i],
-            device_id={"mp": lax.rem(column + k, mp)},
-            device_id_type=MESH,
-        )
-
-    for k in range(1, mp):
-        to = lax.rem(column + k, mp)
-
-        def send_piece(i, carry, k=k, to=to):
-            partial_send[k, i] = product(pl.multiple_of(to * share + i * piece, piece))
-            h_copy(k, i).start()
-            return carry
-
-        lax.fori_loop(0, PIECES, send_piece, 0)
-
-    for k in range(1, seq):
-        r_copy(k).start()
-    got_reply[own_rows, :] = reply[own_rows, :]
 
     row = lax.broadcasted_iota(jnp.int32, (dec, dec), 0)
     col = lax.broadcasted_iota(jnp.int32, (dec, dec), 1)
@@ -369,15 +281,99 @@
         position = jnp.where(lane == head, total, position)
     pos_seq[me] = position
 
-    def keep_piece(i, carry):
-        partial_got[column, i] = product(pl.multiple_of(column * share + i * piece, piece))
+    kv_acc[...] = jnp.zeros_like(kv_acc)
+    for copy in incoming[6:]:
+        copy.wait()
+
+    def project(n, carry):
+        w_copy(n).wait()
+        rows = pl.ds(pl.multiple_of(n * STAGE, STAGE), STAGE)
+        part = jnp.swapaxes(stage[n], 0, 1)
+        w_buf[:, rows, :] = part
+        left = hidden[:, rows]
+        kv_acc[0] += nn(left, part[0])
+        kv_acc[1] += nn(left, part[1])
+
+        @pl.when(n == EARLY)
+        def _():
+            pl.semaphore_wait(barrier, seq - 1 + others - 1)
+            for k in range(1, seq):
+                x_copy(k).start()
+            for k in range(1, seq):
+                p_copy(k).start()
+
         return carry
 
-    lax.fori_loop(0, PIECES - 1, keep_piece, 0)
+    lax.fori_loop(0, steps, project, 0)
+    kv_buf[...] = kv_acc[...].astype(jnp.bfloat16)
 
     for k in range(1, seq):
-        p_copy(k).start()
-    lax.fori_loop(PIECES - 1, PIECES, keep_piece, 0)
+        x_copy(k).wait()
+
+    row = lax.broadcasted_iota(jnp.int32, (dec, enc), 0)
+    col = lax.broadcasted_iota(jnp.int32, (dec, enc), 1)
+    home = jnp.zeros((dec, enc), jnp.int32)
+    offset = jnp.int32(0)
+    for e in range(seq):
+        home = jnp.where(col >= offset, homes[e], home)
+        offset = offset + lengths[e]
+    allowed = (row >> 3) == home
+    query_pos = (row >> 3) * dec + me * TGT_MAX + (row & 7)
+    key_pos = me * enc + col
+    base = scramble(seed[0] + group * 104729)
+    blank = jnp.zeros((dec, enc), jnp.float32)
+    for h in range(heads):
+        cols = slice(h * HEAD, (h + 1) * HEAD)
+        head = column * heads + h
+        both = got[:, cols]
+        key, val = kv_buf[0, :, cols], kv_buf[1, :, cols]
+        probs = softmax(jnp.where(allowed, pick(nt(both, key), 0) * factor, -1e30))
+        keep = keep_table(base, head, query_pos, key_pos)
+        weights = probs * keep
+        dprobs = pick(nt(both, val), 1) * keep
+        delta = jnp.sum(probs * dprobs, axis=-1, keepdims=True)
+        scaled = probs * (dprobs - delta) * factor
+        grad_buf[0, :, cols] = tn(mix(scaled, blank).astype(jnp.bfloat16), both).astype(
+            jnp.bfloat16
+        )
+        grad_buf[1, :, cols] = tn(mix(blank, weights).astype(jnp.bfloat16), both).astype(
+            jnp.bfloat16
+        )
+        reply[:, cols] = mix(
+            nn(weights.astype(jnp.bfloat16), val), nn(scaled.astype(jnp.bfloat16), key)
+        ).astype(jnp.bfloat16)
+
+    share = model // mp
+    piece = share // PIECES
+
+    def product(begin):
+        rows = pl.ds(begin, piece)
+        total = nt(grad_buf[0], w_buf[0, rows, :]) + nt(grad_buf[1], w_buf[1, rows, :])
+        return total.astype(jnp.bfloat16)
+
+    def h_copy(k, i):
+        return pltpu.make_async_remote_copy(
+            src_ref=partial_send.at[k, i],
+            dst_ref=partial_got.at[column, i],
+            send_sem=h_send.at[k, i],
+            recv_sem=h_recv.at[k, i],
+            device_id={"mp": lax.rem(column + k, mp)},
+            device_id_type=MESH,
+        )
+
+    for k in range(1, seq):
+        r_copy(k).start()
+    for k in range(1, mp):
+        to = lax.rem(column + k, mp)
+
+        def send_piece(i, carry, k=k, to=to):
+            partial_send[k, i] = product(pl.multiple_of(to * share + i * piece, piece))
+            h_copy(k, i).start()
+            return carry
+
+        lax.fori_loop(0, PIECES, send_piece, 0)
+
+    got_reply[own_rows, :] = reply[own_rows, :]
     for k in range(1, seq):
         p_copy(k).wait()
     total = pos_seq[0]
@@ -385,6 +381,17 @@
         total = total + pos_seq[s]
     pos_all[mine] = total
 
+    def share_total(k, carry):
+        a_copy(k).start()
+        return carry
+
+    lax.fori_loop(1, others, share_total, 0)
+
+    def keep_piece(i, carry):
+        partial_got[column, i] = product(pl.multiple_of(column * share + i * piece, piece))
+        return carry
+
+    lax.fori_loop(0, PIECES, keep_piece, 0)
     for k in range(1, seq):
         r_copy(k).wait()
     back = got_reply[...].astype(jnp.float32)
@@ -392,11 +399,15 @@
     planes[3] = pick(back, 1).astype(jnp.bfloat16)
     decoder_grads[...] = jnp.swapaxes(planes[...], 0, 1)
 
-    def share_total(k, carry):
-        a_copy(k).start()
+    def take_total(k, carry):
+        a_copy(k).wait()
         return carry
 
-    lax.fori_loop(1, others, share_total, 0)
+    lax.fori_loop(1, others, take_total, 0)
+    total = pos_all[0]
+    for m in range(1, others):
+        total = total + pos_all[m]
+    position_out[...] = total[:, : position_out.shape[1]]
 
     for i in range(PIECES):
         for k in range(1, mp):
@@ -406,23 +417,12 @@
             total = total + partial_got[m, i].astype(jnp.float32)
         hidden_out[:, i * piece : (i + 1) * piece] = total.astype(jnp.bfloat16)
 
-    def take_total(k, carry):
-        a_copy(k).wait()
-        return carry
-
-    lax.fori_loop(1, others, take_total, 0)
-    total = pos_all[0]
-    for m in range(1, others):
-        total = total + pos_all[m]
-    position_out[...] = total
-
 
 def deliver(*refs):
     taken, given, done = refs[:5], refs[5:10], refs[10]
-    copies = [pltpu.make_async_copy(taken[i], given[i], done.at[i]) for i in range(4)]
+    copies = [pltpu.make_async_copy(taken[i], given[i], done.at[i]) for i in range(5)]
     for copy in copies:
         copy.start()
-    given[4][...] = taken[4][:, : given[4].shape[1]]
     for copy in copies:
         copy.wait()
 
@@ -455,7 +455,7 @@
         jax.ShapeDtypeStruct((dec, features), half),
         jax.ShapeDtypeStruct((dec, 4, features), half),
         jax.ShapeDtypeStruct((enc, share), half),
-        jax.ShapeDtypeStruct((TGT_MAX, 128), jnp.float32),
+        jax.ShapeDtypeStruct(position_bias.shape, jnp.float32),
     ]
     results = pl.pallas_call(
         functools.partial(kernel, sizes),
@@ -472,7 +472,7 @@
             pltpu.VMEM((3, dec, features), half),
             pltpu.VMEM((dec, features), half),
             pltpu.VMEM((dec, 2, features), half),
-            pltpu.VMEM((DEPTH, STAGE, 2, features), half),
+            pltpu.VMEM((model // STAGE, STAGE, 2, features), half),
             pltpu.VMEM((2, model, features), half),
             pltpu.VMEM((2, enc, features), jnp.float32),
             pltpu.VMEM((2, enc, features), half),
@@ -487,7 +487,7 @@
             pltpu.VMEM((mp, PIECES, enc, share // PIECES), half),
             pltpu.VMEM((seq, TGT_MAX, 128), jnp.float32),
             pltpu.VMEM((others, TGT_MAX, 128), jnp.float32),
-            dma((DEPTH,)),
+            dma((model // STAGE,)),
             dma((seq,)),
             dma((seq,)),
             dma((seq,)),
@@ -516,13 +516,12 @@
         cross_query[0],
         cotangents[0],
     )
-    shapes[4] = jax.ShapeDtypeStruct(position_bias.shape, jnp.float32)
     self_out, cross_out, decoder_grads, hidden_out, position_out = pl.pallas_call(
         deliver,
         out_shape=tuple(shapes),
         in_specs=[vmem] * 5,
-        out_specs=(hbm,) * 4 + (vmem,),
-        scratch_shapes=[dma((4,))],
+        out_specs=(hbm,) * 5,
+        scratch_shapes=[dma((5,))],
         compiler_params=pltpu.CompilerParams(vmem_limit_bytes=67043328),
         name="deliver",
     )(*results)

time: 39 us -> 36.6 us (0.938)
  the two profiles are of different devices: /device:TPU:0 before, /device:TPU:13 now
where the time goes in v1:
time: 36.6 us; the launch traced here: 36.5 us
  Pallas kernels  35.2 us (96%)
  between operations  1.29 us (4%)
    pallas_call x1, Pallas kernels, body(): pl.pallas_call(functools.partial(kernel, sizes), out_shape=tuple(shapes),...  32.8 us
    pallas_call x1, Pallas kernels, body(): pl.pallas_call(deliver, out_shape=tuple(shapes), in_specs=[vmem] * 5, out...  2.37 us

profile of v1, /device:TPU:13, one launch (start us, length us, event | category | flops | bytes accessed | tf_op | source)
XLA Modules:
  0.0 36.5 jit_solution(13495760324209464515)
XLA Ops:
  1.3 32.8 %fused_layer.1 = (bf16[64,1024]{1,0:T(8,128)(2,1)}, bf16[64,1024]{1,0:T(8,128)(2,1)}, bf16[64,4,1024]{2,1,0:T(4,128)(2,1)}, bf16[112,2048]{1,0:T(8,128)(2,1)}, f32[8,8]{1,0:T(8,128)}) custom-call(s32[8]{0:T(128)} %bitcast.17, s32[8]{0:T(128)} %bitcast.18, s32[8]{0:T(128)} %bitcast.19, s32[1]{0:T(128)S(6)} %copy.15.seed_in, f32[8,8]{1,0:T(8,128)} %bias_in.1, ...), custom_call_target="tpu_custom_call" | custom-call | tf_op jit(solution)/shard_map/fused_layer/pallas_call | solution.py:460
  34.1 2.4 %deliver.1 = (bf16[64,1024]{1,0:T(8,128)(2,1)}, bf16[64,1024]{1,0:T(8,128)(2,1)}, bf16[64,4,1024]{2,1,0:T(4,128)(2,1)}, bf16[112,2048]{1,0:T(8,128)(2,1)}, f32[8,8]{1,0:T(8,128)}) custom-call(bf16[64,1024]{1,0:T(8,128)(2,1)} %get-tuple-element.15.refs_0_, bf16[64,1024]{1,0:T(8,128)(2,1)} %get-tuple-element.16.refs_1_, ...), custom_call_target="tpu_custom_call" | custom-call | tf_op jit(solution)/shard_map/deliver/pallas_call | solution.py:519

commit v2 on v1

--- a/solution.py
+++ b/solution.py
@@ -11,7 +11,8 @@
 TGT_MAX = 8
 PIECES = 8
 STAGE = 256
-EARLY = 7
+GROUP = 4
+EARLY = 0
 
 MESH = pl.DeviceIdType.MESH
 drop_limit = 6554
@@ -285,16 +286,18 @@
     for copy in incoming[6:]:
         copy.wait()
 
-    def project(n, carry):
+    wide = GROUP * STAGE
+
+    def arrange(n, carry):
         w_copy(n).wait()
         rows = pl.ds(pl.multiple_of(n * STAGE, STAGE), STAGE)
-        part = jnp.swapaxes(stage[n], 0, 1)
-        w_buf[:, rows, :] = part
-        left = hidden[:, rows]
-        kv_acc[0] += nn(left, part[0])
-        kv_acc[1] += nn(left, part[1])
-
-        @pl.when(n == EARLY)
+        w_buf[:, rows, :] = jnp.swapaxes(stage[n], 0, 1)
+        return carry
+
+    def project(g, carry):
+        lax.fori_loop(g * GROUP, (g + 1) * GROUP, arrange, 0)
+
+        @pl.when(g == EARLY)
         def _():
             pl.semaphore_wait(barrier, seq - 1 + others - 1)
             for k in range(1, seq):
@@ -302,9 +305,13 @@
             for k in range(1, seq):
                 p_copy(k).start()
 
-        return carry
-
-    lax.fori_loop(0, steps, project, 0)
+        rows = pl.ds(pl.multiple_of(g * wide, wide), wide)
+        left = hidden[:, rows]
+        kv_acc[0] += nn(left, w_buf[0, rows, :])
+        kv_acc[1] += nn(left, w_buf[1, rows, :])
+        return carry
+
+    lax.fori_loop(0, model // wide, project, 0)
     kv_buf[...] = kv_acc[...].astype(jnp.bfloat16)
 
     for k in range(1, seq):

time: 36.6 us -> 32.7 us (0.89)
  Pallas kernels: 35.2 us -> 31.3 us
    pallas_call x1, Pallas kernels: 32.8 us -> 28.9 us  [body(): pl.pallas_call(functools.partial(kernel, sizes), out_shape=tuple(shapes),...]
where the time goes in v2:
time: 32.7 us; the launch traced here: 32.5 us
  Pallas kernels  31.3 us (96%)
  between operations  1.29 us (4%)
    pallas_call x1, Pallas kernels, body(): pl.pallas_call(functools.partial(kernel, sizes), out_shape=tuple(shapes),...  28.9 us
    pallas_call x1, Pallas kernels, body(): pl.pallas_call(deliver, out_shape=tuple(shapes), in_specs=[vmem] * 5, out...  2.37 us

profile of v2, /device:TPU:13, one launch (start us, length us, event | category | flops | bytes accessed | tf_op | source)
XLA Modules:
  0.0 32.5 jit_solution(6143663709561457157)
XLA Ops:
  1.3 28.9 %fused_layer.1 = (bf16[64,1024]{1,0:T(8,128)(2,1)}, bf16[64,1024]{1,0:T(8,128)(2,1)}, bf16[64,4,1024]{2,1,0:T(4,128)(2,1)}, bf16[112,2048]{1,0:T(8,128)(2,1)}, f32[8,8]{1,0:T(8,128)}) custom-call(s32[8]{0:T(128)} %bitcast.17, s32[8]{0:T(128)} %bitcast.18, s32[8]{0:T(128)} %bitcast.19, s32[1]{0:T(128)S(6)} %copy.15.seed_in, f32[8,8]{1,0:T(8,128)} %bias_in.1, ...), custom_call_target="tpu_custom_call" | custom-call | tf_op jit(solution)/shard_map/fused_layer/pallas_call | solution.py:467
  30.2 2.4 %deliver.1 = (bf16[64,1024]{1,0:T(8,128)(2,1)}, bf16[64,1024]{1,0:T(8,128)(2,1)}, bf16[64,4,1024]{2,1,0:T(4,128)(2,1)}, bf16[112,2048]{1,0:T(8,128)(2,1)}, f32[8,8]{1,0:T(8,128)}) custom-call(bf16[64,1024]{1,0:T(8,128)(2,1)} %get-tuple-element.15.refs_0_, bf16[64,1024]{1,0:T(8,128)(2,1)} %get-tuple-element.16.refs_1_, ...), custom_call_target="tpu_custom_call" | custom-call | tf_op jit(solution)/shard_map/deliver/pallas_call | solution.py:526

commit v3 on v2

--- a/solution.py
+++ b/solution.py
@@ -106,6 +106,7 @@
     a_send,
     a_recv,
     in_sem,
+    keeps,
 ):
     seq, mp, dp = sizes
     me = lax.axis_index("seq")
@@ -302,8 +303,6 @@
             pl.semaphore_wait(barrier, seq - 1 + others - 1)
             for k in range(1, seq):
                 x_copy(k).start()
-            for k in range(1, seq):
-                p_copy(k).start()
 
         rows = pl.ds(pl.multiple_of(g * wide, wide), wide)
         left = hidden[:, rows]
@@ -313,9 +312,6 @@
 
     lax.fori_loop(0, model // wide, project, 0)
     kv_buf[...] = kv_acc[...].astype(jnp.bfloat16)
-
-    for k in range(1, seq):
-        x_copy(k).wait()
 
     row = lax.broadcasted_iota(jnp.int32, (dec, enc), 0)
     col = lax.broadcasted_iota(jnp.int32, (dec, enc), 1)
@@ -328,6 +324,13 @@
     query_pos = (row >> 3) * dec + me * TGT_MAX + (row & 7)
     key_pos = me * enc + col
     base = scramble(seed[0] + group * 104729)
+    for h in range(heads):
+        keeps[h] = keep_table(base, column * heads + h, query_pos, key_pos)
+    for k in range(1, seq):
+        x_copy(k).wait()
+    for k in range(1, seq):
+        p_copy(k).start()
+
     blank = jnp.zeros((dec, enc), jnp.float32)
     for h in range(heads):
         cols = slice(h * HEAD, (h + 1) * HEAD)
@@ -335,7 +338,7 @@
         both = got[:, cols]
         key, val = kv_buf[0, :, cols], kv_buf[1, :, cols]
         probs = softmax(jnp.where(allowed, pick(nt(both, key), 0) * factor, -1e30))
-        keep = keep_table(base, head, query_pos, key_pos)
+        keep = keeps[h]
         weights = probs * keep
         dprobs = pick(nt(both, val), 1) * keep
         delta = jnp.sum(probs * dprobs, axis=-1, keepdims=True)
@@ -368,8 +371,6 @@
             device_id_type=MESH,
         )
 
-    for k in range(1, seq):
-        r_copy(k).start()
     for k in range(1, mp):
         to = lax.rem(column + k, mp)
 
@@ -378,7 +379,11 @@
             h_copy(k, i).start()
             return carry
 
-        lax.fori_loop(0, PIECES, send_piece, 0)
+        lax.fori_loop(0, 1, send_piece, 0)
+        if k == 1:
+            for q in range(1, seq):
+                r_copy(q).start()
+        lax.fori_loop(1, PIECES, send_piece, 0)
 
     got_reply[own_rows, :] = reply[own_rows, :]
     for k in range(1, seq):
@@ -506,6 +511,7 @@
             dma((others,)),
             dma((others,)),
             dma((9,)),
+            pltpu.VMEM((features // HEAD, dec, enc), jnp.float32),
         ],
         compiler_params=pltpu.CompilerParams(
             collective_id=0, has_side_effects=True, vmem_limit_bytes=67043328

time: 32.7 us -> 32.1 us (0.982)
  Pallas kernels: 31.3 us -> 30.7 us
    pallas_call x1, Pallas kernels: 28.9 us -> 28.3 us  [body(): pl.pallas_call(functools.partial(kernel, sizes), out_shape=tuple(shapes),...]
where the time goes in v3:
time: 32.1 us; the launch traced here: 32 us
  Pallas kernels  30.7 us (96%)
  between operations  1.29 us (4%)
    pallas_call x1, Pallas kernels, body(): pl.pallas_call(functools.partial(kernel, sizes), out_shape=tuple(shapes),...  28.3 us
    pallas_call x1, Pallas kernels, body(): pl.pallas_call(deliver, out_shape=tuple(shapes), in_specs=[vmem] * 5, out...  2.37 us

profile of v3, /device:TPU:13, one launch (start us, length us, event | category | flops | bytes accessed | tf_op | source)
XLA Modules:
  0.0 32.0 jit_solution(9800960690642529810)
XLA Ops:
  1.3 28.3 %fused_layer.1 = (bf16[64,1024]{1,0:T(8,128)(2,1)}, bf16[64,1024]{1,0:T(8,128)(2,1)}, bf16[64,4,1024]{2,1,0:T(4,128)(2,1)}, bf16[112,2048]{1,0:T(8,128)(2,1)}, f32[8,8]{1,0:T(8,128)}) custom-call(s32[8]{0:T(128)} %bitcast.17, s32[8]{0:T(128)} %bitcast.18, s32[8]{0:T(128)} %bitcast.19, s32[1]{0:T(128)S(6)} %copy.15.seed_in, f32[8,8]{1,0:T(8,128)} %bias_in.1, ...), custom_call_target="tpu_custom_call" | custom-call | tf_op jit(solution)/shard_map/fused_layer/pallas_call | solution.py:472
  29.6 2.4 %deliver.1 = (bf16[64,1024]{1,0:T(8,128)(2,1)}, bf16[64,1024]{1,0:T(8,128)(2,1)}, bf16[64,4,1024]{2,1,0:T(4,128)(2,1)}, bf16[112,2048]{1,0:T(8,128)(2,1)}, f32[8,8]{1,0:T(8,128)}) custom-call(bf16[64,1024]{1,0:T(8,128)(2,1)} %get-tuple-element.15.refs_0_, bf16[64,1024]{1,0:T(8,128)(2,1)} %get-tuple-element.16.refs_1_, ...), custom_call_target="tpu_custom_call" | custom-call | tf_op jit(solution)/shard_map/deliver/pallas_call | solution.py:532
